TPU v7x, 32 devices: a whole 2x2x4 slice. The times are simulated.
32 devices in a mesh: dap: 8 (over y, x, core), seq: 4 (over z).
Axes of the slice: x: 2, y: 2, z: 4, core: 2. Of those that a mesh axis runs over, the one named last changes fastest.
Arguments:
- homolog_tensor: bfloat16 [8, 32, 256], P('dap', 'seq'), may hold values from -6 to 6
- pair_features: bfloat16 [32, 32, 128], P('seq', 'dap'), may hold values from -6 to 6
- entry_real_mask: int32 [8, 32], P('dap', 'seq'), may hold values 0 or 1
- chain_ids: int32 [32], replicated, may hold values from 0 to 3, never falling along the last dimension, each value on 1 to 16 neighbouring positions
- horizontal_matrices: bfloat16 [256, 1024], replicated, may hold values from -0.375 to 0.375
- horizontal_projector: bfloat16 [256, 256], replicated, may hold values from -0.375 to 0.375
- bias_proj: float32 [128, 8], replicated, may hold values from -35.35534 to 35.35534
- chain_bias: float32 [2, 8], replicated, may hold values from -4 to 4
- column_proj: bfloat16 [256, 1024], replicated, may hold values from -12.5 to 12.5
- vertical_projector: bfloat16 [256, 256], replicated, may hold values from -0.375 to 0.375
- expansion_matrix: bfloat16 [256, 1024], replicated, may hold values from -0.375 to 0.375
- contraction_matrix: bfloat16 [1024, 256], replicated, may hold values from -0.1875 to 0.1875
Outputs:
- updated: bfloat16 [8, 32, 256], P('dap', 'seq')
Inputs may be any that keep to these rules, and one draw needn't show every extreme that they name: `chain_ids`: chain numbers never fall along the residues.
All inputs are finite; a program needn't handle non-finite values. No bound on the sum of `entry_real_mask` on one device may be relied on, other than what follows from the above.
Results may differ from a plain program's by a relative error of at most 0.013.
The roundings to bfloat16 on the way count: a program that leaves them out, or rounds other values in their place, can miss the bound.
Values may be sent and summed in bfloat16 or wider, within the bound.
No kernel may reach another device: no remote copies, remote signals or barrier semaphores. Data moves between devices by JAX's collectives and lax.ppermute only.
A program may use at most 64 MiB of HBM per device.

v0:
```python
import jax
import jax.numpy as jnp
from jax import lax
from jax.sharding import PartitionSpec as P

HEAD_TOTAL = 8
HEAD_DEPTH = 32
epsilon = 1e-05


def layer_norm(inputs):
    center = inputs - jnp.mean(inputs, axis=-1, keepdims=True)
    spread = jnp.mean(center * center, axis=-1, keepdims=True)
    return center * lax.rsqrt(spread + epsilon)


def attend(queries, key_part, value_part, keep_mask, bias_term):
    scores = jnp.einsum(
        "ihd,jhd->hij", queries, key_part, preferred_element_type=jnp.float32
    ) * HEAD_DEPTH ** (-0.5)
    if bias_term is not None:
        scores = scores + bias_term.astype(jnp.float32)
    scores = jnp.where(keep_mask[None, None, :] > 0, scores, -1000000000.0)
    weights = jax.nn.softmax(scores, axis=-1).astype(jnp.bfloat16)
    return jnp.einsum("hij,jhd->ihd", weights, value_part, preferred_element_type=jnp.float32)


def column_update(
    column, keep_column, column_proj, vertical_projector, expansion_matrix, contraction_matrix
):
    expanded_dimension = HEAD_TOTAL * HEAD_DEPTH
    standardized = layer_norm(column.astype(jnp.float32)).astype(jnp.bfloat16)
    projected = jnp.dot(standardized, column_proj, preferred_element_type=jnp.float32).astype(
        jnp.bfloat16
    )
    queries = projected[:, :expanded_dimension].reshape(-1, HEAD_TOTAL, HEAD_DEPTH)
    key_part = projected[:, expanded_dimension : 2 * expanded_dimension].reshape(
        -1, HEAD_TOTAL, HEAD_DEPTH
    )
    value_part = projected[:, 2 * expanded_dimension : 3 * expanded_dimension].reshape(
        -1, HEAD_TOTAL, HEAD_DEPTH
    )
    attended = attend(queries, key_part, value_part, keep_column, None).reshape(
        -1, expanded_dimension
    )
    sigmoid_scaled = (
        jax.nn.sigmoid(projected[:, 3 * expanded_dimension :].astype(jnp.float32)) * attended
    ).astype(jnp.bfloat16)
    mixed = column.astype(jnp.float32) + jnp.dot(
        sigmoid_scaled, vertical_projector, preferred_element_type=jnp.float32
    )
    inner = jnp.maximum(
        jnp.dot(
            layer_norm(mixed).astype(jnp.bfloat16),
            expansion_matrix,
            preferred_element_type=jnp.float32,
        ),
        0.0,
    ).astype(jnp.bfloat16)
    return (mixed + jnp.dot(inner, contraction_matrix, preferred_element_type=jnp.float32)).astype(
        jnp.bfloat16
    )


def body(
    homolog_tensor,
    pair_features,
    entry_real_mask,
    chain_ids,
    horizontal_matrices,
    horizontal_projector,
    bias_proj,
    chain_bias,
    column_proj,
    vertical_projector,
    expansion_matrix,
    contraction_matrix,
):
    row_count, local_residues, channels = homolog_tensor.shape
    expanded_dimension = HEAD_TOTAL * HEAD_DEPTH
    dap_count = lax.axis_size("dap")
    pair_rows, pair_columns, pair_width = pair_features.shape
    normed_pair = layer_norm(pair_features.astype(jnp.float32))
    projected_pair = jnp.einsum(
        "ijc,ch->hij", normed_pair, bias_proj, precision=lax.Precision.HIGHEST
    )
    row_chain = lax.dynamic_slice_in_dim(chain_ids, lax.axis_index("seq") * pair_rows, pair_rows)
    column_chain = lax.dynamic_slice_in_dim(
        chain_ids, lax.axis_index("dap") * pair_columns, pair_columns
    )
    same_chain = (row_chain[:, None] == column_chain[None, :]).astype(jnp.float32)
    chain_term = chain_bias[0][:, None, None] * same_chain + chain_bias[1][:, None, None] * (
        1.0 - same_chain
    )
    local_bias = (projected_pair + chain_term).astype(jnp.bfloat16)
    pair_bias = lax.all_gather(local_bias, "dap", axis=2, tiled=True)
    standardized = layer_norm(homolog_tensor.astype(jnp.float32)).astype(jnp.bfloat16)
    flat = standardized.reshape(-1, channels)
    keep_mask = entry_real_mask.astype(jnp.bfloat16)
    projected = (
        jnp.dot(flat, horizontal_matrices, preferred_element_type=jnp.float32)
        .astype(jnp.bfloat16)
        .reshape(row_count, local_residues, 4 * expanded_dimension)
    )
    queries = projected[..., :expanded_dimension]
    gating = projected[..., 3 * expanded_dimension :]
    key_values, keep_all = (
        lax.all_gather(
            projected[..., expanded_dimension : 3 * expanded_dimension], "seq", axis=1, tiled=True
        ),
        lax.all_gather(keep_mask, "seq", axis=1, tiled=True),
    )

    def one_row(inputs_row):
        row_queries, row_pairs, row_keep = inputs_row
        key_part = row_pairs[:, :expanded_dimension].reshape(-1, HEAD_TOTAL, HEAD_DEPTH)
        value_part = row_pairs[:, expanded_dimension:].reshape(-1, HEAD_TOTAL, HEAD_DEPTH)
        return attend(
            row_queries.reshape(local_residues, HEAD_TOTAL, HEAD_DEPTH),
            key_part,
            value_part,
            row_keep,
            pair_bias,
        ).reshape(local_residues, expanded_dimension)

    attended = lax.map(one_row, (queries, key_values, keep_all))
    sigmoid_scaled = (jax.nn.sigmoid(gating.astype(jnp.float32)) * attended).astype(jnp.bfloat16)
    row_result = jnp.dot(
        sigmoid_scaled.reshape(-1, expanded_dimension),
        horizontal_projector,
        preferred_element_type=jnp.float32,
    ).reshape(row_count, local_residues, channels)
    updated_rows = (homolog_tensor.astype(jnp.float32) + row_result).astype(jnp.bfloat16)
    per_device = local_residues // dap_count
    blocks = updated_rows.reshape(row_count, dap_count, per_device, channels)
    keep_blocks = keep_mask.reshape(row_count, dap_count, per_device)

    def single_column(inputs_col):
        return column_update(
            inputs_col[0],
            inputs_col[1],
            column_proj,
            vertical_projector,
            expansion_matrix,
            contraction_matrix,
        )

    column_block = lax.all_to_all(blocks, "dap", split_axis=1, concat_axis=0, tiled=True)
    column_keep = lax.all_to_all(keep_blocks, "dap", split_axis=1, concat_axis=0, tiled=True)
    inputs_col = (jnp.moveaxis(column_block[:, 0], 1, 0), jnp.moveaxis(column_keep[:, 0], 1, 0))
    output_list = lax.map(single_column, inputs_col)
    mixed = jnp.moveaxis(output_list, 0, 1)[:, None]
    returned = lax.all_to_all(mixed, "dap", split_axis=0, concat_axis=1, tiled=True)
    return returned.reshape(row_count, local_residues, channels)


def solution(mesh):
    placed = (
        P("dap", "seq", None),
        P("seq", "dap", None),
        P("dap", "seq"),
        P(),
        P(),
        P(),
        P(),
        P(),
        P(),
        P(),
        P(),
        P(),
    )
    return jax.shard_map(
        body, mesh=mesh, in_specs=placed, out_specs=P("dap", "seq", None), check_vma=False
    )
```

profile of v0, /device:TPU:0, one launch (start us, length us, event | category | flops | bytes accessed | tf_op | source)
XLA Modules:
  0.0 71.7 jit_solution(17577258312015481253)
XLA Ops:
  0.0 0.7 convert_bitcast_fusion.1
  0.7 0.7 copy.49
  1.4 5.2 %all-to-all-start.1 = ((bf16[1,8,1]{2,0,1:T(2,128)(2,1)}), bf16[1,8,1]{2,0,1:T(2,128)(2,1)S(1)}, u32[]{:S(2)}, u32[]{:S(2)}) async-start(bf16[1,8,1]{2,0,1:T(2,128)(2,1)} %copy.49), calls=%async_computation.1 | async-start | bytes 8192 | tf_op jit(solution)/shard_map/all_to_all | solution.py:149
  6.6 0.7 copy-done.12
  7.6 0.5 copy-done.6
  8.3 0.2 fusion.12
  8.6 0.6 copy-done.7
  9.2 0.7 copy-done.5
  10.2 0.6 copy-done.9
  10.8 0.7 copy-done.11
  11.7 9.7 %all_gather.11 = bf16[8,8,32]{1,0,2:T(8,128)(2,1)S(1)} all-gather(bf16[8,8,4]{1,0,2:T(8,128)(2,1)S(1)} %copy.43), channel_id=1, replica_groups=mesh['dap'=8,'seq'=4] {'dap'}, dimensions={2}, use_global_device_ids=true | all-gather | bytes 4608 | tf_op jit(solution)/shard_map/all_gather | solution.py:96
  21.6 0.6 slice-done
  22.2 13.4 %all_gather.9 = bf16[1,32,512]{2,1,0:T(8,128)(2,1)S(1)} all-gather(bf16[1,8,512]{2,1,0:T(8,128)(2,1)S(1)} %slice-done), channel_id=1, replica_groups=mesh['dap'=8,'seq'=4] {'seq'}, dimensions={1}, use_global_device_ids=true | all-gather | bytes 40960 | tf_op jit(solution)/shard_map/all_gather | solution.py:108
  35.7 0.6 slice-done.1
  36.3 0.6 dynamic-slice
  37.6 0.2 dynamic-update-slice
  37.8 11.7 %all-reduce = bf16[32]{0:T(256)(128)(2,1)S(1)} all-reduce(bf16[32]{0:T(256)(128)(2,1)S(1)} %dynamic-update-slice), channel_id=1, replica_groups=mesh['dap'=8,'seq'=4] {'seq'}, use_global_device_ids=true, to_apply=%add | all-reduce | flops 32 | bytes 128
  50.0 0.3 convolution_bitcast_fusion.1
  50.3 0.5 copy-done.3
  51.2 0.6 broadcast.220
  51.8 0.7 %reduce.5 = bf16[8,256]{1,0:T(8,128)(2,1)S(1)} reduce(bf16[8,1,1,256]{3,2,1,0:T(2,128)(2,1)S(1)} %bitcast.75, bf16[]{:T(256)} %broadcast.220), dimensions={1,2}, to_apply=%bitcast.73.reduce_sub_computation | reduce | bytes 8194
  52.5 0.6 reshape.228
  53.1 3.3 %all-to-all-start = ((bf16[8,2,128]{2,1,0:T(2,128)(2,1)}), bf16[8,2,128]{2,1,0:T(2,128)(2,1)S(1)}, u32[]{:S(2)}, u32[]{:S(2)}) async-start(bf16[8,2,128]{2,1,0:T(2,128)(2,1)} %reshape.228), calls=%async_computation | async-start | bytes 8192 | tf_op jit(solution)/shard_map/all_to_all | solution.py:148
  56.4 0.2 compare_reduce_fusion
  56.6 4.3 %all-to-all-done = bf16[8,2,128]{2,1,0:T(2,128)(2,1)S(1)} async-done(((bf16[8,2,128]{2,1,0:T(2,128)(2,1)}), bf16[8,2,128]{2,1,0:T(2,128)(2,1)S(1)}, u32[]{:S(2)}, u32[]{:S(2)}) %all-to-all-start) | async-done | bytes 4128 | tf_op jit(solution)/shard_map/all_to_all | solution.py:148
  61.3 0.2 convolution_convert_fusion
  62.1 0.2 convolution_bitcast_fusion
  62.4 0.3 fusion.72
  62.9 0.4 fusion.18
  63.3 0.7 reduce.6
  64.0 7.1 %all_to_all.12 = bf16[8,2,128]{2,1,0:T(2,128)(2,1)S(1)} all-to-all(bf16[8,2,128]{2,1,0:T(2,128)(2,1)S(1)} %reshape.230), channel_id=1, replica_groups=mesh['dap'=8,'seq'=4] {'dap'}, dimensions={0} | all-to-all | bytes 8192 | tf_op jit(solution)/shard_map/all_to_all | solution.py:153
  71.1 0.6 copy.83
  (71 shorter events, 3.5 us)
Async XLA Ops:
  0.0 8.3 %copy-start = (bf16[256,1024]{1,0:T(8,128)(2,1)S(1)}, bf16[256,1024]{1,0:T(8,128)(2,1)}, u32[]{:S(2)}) copy-start(bf16[256,1024]{1,0:T(8,128)(2,1)} %param.16) | copy-start | bytes 1572868
  1.4 51.7 %all-to-all-start.1 = ((bf16[1,8,1]{2,0,1:T(2,128)(2,1)}), bf16[1,8,1]{2,0,1:T(2,128)(2,1)S(1)}, u32[]{:S(2)}, u32[]{:S(2)}) async-start(bf16[1,8,1]{2,0,1:T(2,128)(2,1)} %copy.49), calls=%async_computation.1 | async-start | bytes 8192 | tf_op jit(solution)/shard_map/all_to_all | solution.py:149
  6.6 0.7 copy-start.12
  7.3 0.7 copy-start.6
  8.6 0.6 copy-start.7
  9.2 0.7 copy-start.5
  10.1 0.7 copy-start.9
  10.8 0.7 copy-start.11
  21.5 0.7 slice-start
  35.5 0.8 %copy-start.13 = (u32[32]{0:T(128)S(1)}, u32[32]{0:T(128)}, u32[]{:S(2)}) copy-start(u32[32]{0:T(128)} %constant.98) | copy-start | bytes 388
  35.5 0.7 slice-start.1
  35.5 25.7 %copy-start.10 = (bf16[256,1024]{1,0:T(8,128)(2,1)S(1)}, bf16[256,1024]{1,0:T(8,128)(2,1)}, u32[]{:S(2)}) copy-start(bf16[256,1024]{1,0:T(8,128)(2,1)} %param.20) | copy-start | bytes 1572868
  50.0 0.9 %copy-start.3 = (bf16[256,256]{1,0:T(8,128)(2,1)S(1)}, bf16[256,256]{1,0:T(8,128)(2,1)}, u32[]{:S(2)}) copy-start(bf16[256,256]{1,0:T(8,128)(2,1)} %param.17) | copy-start | bytes 393220
  50.3 0.7 %copy-start.8 = (bf16[1,8,1024]{2,1,0:T(8,128)(2,1)S(1)}, bf16[1,8,1024]{2,1,0:T(8,128)(2,1)}, u32[]{:S(2)}) copy-start(bf16[1,8,1024]{2,1,0:T(8,128)(2,1)} %copy-done.7) | copy-start | bytes 49156
  53.1 7.9 %all-to-all-start = ((bf16[8,2,128]{2,1,0:T(2,128)(2,1)}), bf16[8,2,128]{2,1,0:T(2,128)(2,1)S(1)}, u32[]{:S(2)}, u32[]{:S(2)}) async-start(bf16[8,2,128]{2,1,0:T(2,128)(2,1)} %reshape.228), calls=%async_computation | async-start | bytes 8192 | tf_op jit(solution)/shard_map/all_to_all | solution.py:148
  61.3 1.1 %copy-start.4 = (bf16[256,256]{1,0:T(8,128)(2,1)S(1)}, bf16[256,256]{1,0:T(8,128)(2,1)}, u32[]{:S(2)}) copy-start(bf16[256,256]{1,0:T(8,128)(2,1)} %param.21) | copy-start | bytes 393220
  61.3 1.6 %copy-start.2 = (bf16[256,1024]{1,0:T(8,128)(2,1)S(1)}, bf16[256,1024]{1,0:T(8,128)(2,1)}, u32[]{:S(2)}) copy-start(bf16[256,1024]{1,0:T(8,128)(2,1)} %param.22) | copy-start | bytes 1572868
  61.5 1.3 %copy-start.1 = (bf16[1024,256]{1,0:T(8,128)(2,1)S(1)}, bf16[1024,256]{1,0:T(8,128)(2,1)}, u32[]{:S(2)}) copy-start(bf16[1024,256]{1,0:T(8,128)(2,1)} %param.23) | copy-start | bytes 1572868
where the time goes:
time: 72.2 us; the launch traced here: 71.7 us
  blocking collectives  41.9 us (58%)
  local copies, waits for them, and re-layouts  9.98 us (14%)
  starting transfers between devices  8.51 us (12%)
  waiting for transfers between devices  4.3 us (6%)
  other arithmetic  3.88 us (5%)
  matrix products  2.23 us (3%)
  between operations  0.87 us (1%)
    all_gather x1, blocking collectives, body(): lax.all_gather(projected[..., expanded_dimension:3 * expanded_dimension],...  13.4 us
    unnamed x1, blocking collectives  11.7 us
    all_gather x1, blocking collectives, body(): pair_bias = lax.all_gather(local_bias, 'dap', axis=2, tiled=True)  9.75 us
    all_to_all x1, blocking collectives, body(): lax.all_to_all(mixed, 'dap', split_axis=0, concat_axis=1, tiled=True)  7.05 us
    unnamed x37, local copies, waits for them, and re-layouts  7.04 us
    all_to_all x1, starting transfers between devices, body(): lax.all_to_all(keep_blocks, 'dap', split_axis=1, concat_axis=0, tiled=True)  5.2 us
    all_to_all x1, waiting for transfers between devices, body(): lax.all_to_all(blocks, 'dap', split_axis=1, concat_axis=0, tiled=True)  4.3 us
    all_to_all x1, starting transfers between devices, body(): lax.all_to_all(blocks, 'dap', split_axis=1, concat_axis=0, tiled=True)  3.31 us
  transfers between devices with their start and end apart: 2, of which 1 were waited for; matrix products, arithmetic and copies ran while one was open for 8% of the time, Pallas kernels for 0%

commit v1 on v0

--- a/solution.py
+++ b/solution.py
@@ -6,6 +6,18 @@
 HEAD_TOTAL = 8
 HEAD_DEPTH = 32
 epsilon = 1e-05
+
+
+def doubled_up(array, axis, dim):
+    ways, here = (lax.axis_size(axis), lax.axis_index(axis))
+    grown, reach = (array, 1)
+    while reach < ways:
+        theirs = lax.ppermute(grown, axis, [(d, d ^ reach) for d in range(ways)])
+        mine_first = jnp.concatenate([grown, theirs], axis=dim)
+        theirs_first = jnp.concatenate([theirs, grown], axis=dim)
+        grown = jnp.where(here & reach == 0, mine_first, theirs_first)
+        reach = 2 * reach
+    return grown
 
 
 def layer_norm(inputs):
@@ -105,9 +117,7 @@
     queries = projected[..., :expanded_dimension]
     gating = projected[..., 3 * expanded_dimension :]
     key_values, keep_all = (
-        lax.all_gather(
-            projected[..., expanded_dimension : 3 * expanded_dimension], "seq", axis=1, tiled=True
-        ),
+        doubled_up(projected[..., expanded_dimension : 3 * expanded_dimension], "seq", 1),
         lax.all_gather(keep_mask, "seq", axis=1, tiled=True),
     )
 

time: 72.2 us -> 62.2 us (0.86)
  blocking collectives: 41.9 us -> 27.8 us
  waiting for transfers between devices: 4.3 us -> 8.9 us
  local copies, waits for them, and re-layouts: 9.98 us -> 7.72 us
  starting transfers between devices: 8.51 us -> 10.2 us
    all_gather x1 -> x0, blocking collectives: 13.4 us -> none  [body(): lax.all_gather(projected[..., expanded_dimension:3 * expanded_dimension],...]
    ppermute x0 -> x2, waiting for transfers between devices: none -> 4.6 us  [doubled_up(): theirs = lax.ppermute(grown, axis, [(d, d ^ reach) for d in range(ways)])]
    ppermute x0 -> x2, starting transfers between devices: none -> 3.19 us  [doubled_up(): theirs = lax.ppermute(grown, axis, [(d, d ^ reach) for d in range(ways)])]
    unnamed x37 -> x39, local copies, waits for them, and re-layouts: 7.04 us -> 5.25 us
    all_to_all x1, starting transfers between devices: 5.2 us -> 3.72 us  [body(): lax.all_to_all(keep_blocks, 'dap', split_axis=1, concat_axis=0, tiled=True)]
    reduce_sum x3, other arithmetic: 0.31 us -> 1.07 us  [layer_norm(): center = inputs - jnp.mean(inputs, axis=-1, keepdims=True)]
    unnamed x1, blocking collectives: 11.7 us -> 11 us
  transfers between devices with their start and end apart: 2 -> 4, of which waited for: 1 -> 2; matrix products, arithmetic and copies ran while one was open for 8% -> 9% of each run, Pallas kernels for 0% -> 0%
where the time goes in v1:
time: 62.2 us; the launch traced here: 61.7 us
  blocking collectives  27.8 us (45%)
  starting transfers between devices  10.2 us (16%)
  waiting for transfers between devices  8.9 us (14%)
  local copies, waits for them, and re-layouts  7.72 us (12%)
  other arithmetic  3.94 us (6%)
  matrix products  2.23 us (4%)
  between operations  0.94 us (2%)
    unnamed x1, blocking collectives  11 us
    all_gather x1, blocking collectives, body(): pair_bias = lax.all_gather(local_bias, 'dap', axis=2, tiled=True)  9.75 us
    all_to_all x1, blocking collectives, body(): lax.all_to_all(mixed, 'dap', split_axis=0, concat_axis=1, tiled=True)  7.05 us
    unnamed x39, local copies, waits for them, and re-layouts  5.25 us
    ppermute x2, waiting for transfers between devices, doubled_up(): theirs = lax.ppermute(grown, axis, [(d, d ^ reach) for d in range(ways)])  4.6 us
    all_to_all x1, waiting for transfers between devices, body(): lax.all_to_all(blocks, 'dap', split_axis=1, concat_axis=0, tiled=True)  4.3 us
    all_to_all x1, starting transfers between devices, body(): lax.all_to_all(keep_blocks, 'dap', split_axis=1, concat_axis=0, tiled=True)  3.72 us
    all_to_all x1, starting transfers between devices, body(): lax.all_to_all(blocks, 'dap', split_axis=1, concat_axis=0, tiled=True)  3.31 us
  transfers between devices with their start and end apart: 4, of which 2 were waited for; matrix products, arithmetic and copies ran while one was open for 9% of the time, Pallas kernels for 0%

profile of v1, /device:TPU:0, one launch (start us, length us, event | category | flops | bytes accessed | tf_op | source)
XLA Modules:
  0.0 61.7 jit_solution(14862820971729234730)
XLA Ops:
  0.0 0.9 %convert_reduce_fusion.1 = f32[8]{0:T(128)S(1)} fusion(bf16[1,8,256]{2,1,0:T(8,128)(2,1)} %param.12), kind=kLoop, calls=%fused_computation.52 | loop fusion | flops 4088 | bytes 4128 | tf_op jit(solution)/shard_map/reduce_sum | solution.py:24
  0.9 0.2 fusion.38
  1.1 0.2 fusion.12
  1.3 3.1 %collective-permute-start = (bf16[1,8,512]{2,1,0:T(8,128)(2,1)S(1)}, bf16[1,8,512]{2,1,0:T(8,128)(2,1)S(1)}, u32[]{:S(2)}, u32[]{:S(2)}) collective-permute-start(bf16[1,8,512]{2,1,0:T(8,128)(2,1)S(1)} %get-tuple-element.45), channel_id=1, source_target_pairs={{0,1},{1,0},{2,3},{3,2},{4,5},{5,4},{6,7},{7,6},{8,9},{9,8},{10,11... | collective-permute-start | bytes 24584 | tf_op jit(solution)/shard_map/ppermute | solution.py:15
  4.4 0.7 %copy.49 = bf16[1,8,1]{2,0,1:T(2,128)(2,1)} copy(bf16[1,8,1]{1,2,0:T(2,128)(2,1)S(1)} %get-tuple-element.56) | data formatting | bytes 32 | tf_op jit(solution)/shard_map/reshape | solution.py:146
  5.1 3.7 %all-to-all-start.1 = ((bf16[1,8,1]{2,0,1:T(2,128)(2,1)}), bf16[1,8,1]{2,0,1:T(2,128)(2,1)S(1)}, u32[]{:S(2)}, u32[]{:S(2)}) async-start(bf16[1,8,1]{2,0,1:T(2,128)(2,1)} %copy.49), calls=%async_computation.1 | async-start | bytes 8192 | tf_op jit(solution)/shard_map/all_to_all | solution.py:159
  8.9 0.6 %copy-done.13 = s32[32]{0:T(128)S(1)} copy-done((s32[32]{0:T(128)S(1)}, s32[32]{0:T(128)}, u32[]{:S(2)}) %copy-start.13) | copy-done | bytes 152
  10.2 0.6 copy-done.9
  10.8 0.7 %copy-done.14 = u32[32]{0:T(128)S(1)} copy-done((u32[32]{0:T(128)S(1)}, u32[32]{0:T(128)}, u32[]{:S(2)}) %copy-start.14) | copy-done | bytes 152
  11.4 0.6 dynamic-slice
  12.7 0.2 dynamic-update-slice
  12.9 11.0 %all-reduce = bf16[32]{0:T(256)(128)(2,1)S(1)} all-reduce(bf16[32]{0:T(256)(128)(2,1)S(1)} %dynamic-update-slice), channel_id=1, replica_groups=mesh['dap'=8,'seq'=4] {'seq'}, use_global_device_ids=true, to_apply=%add | all-reduce | flops 32 | bytes 128
  24.1 9.7 %all_gather.7 = bf16[8,8,32]{1,0,2:T(8,128)(2,1)S(1)} all-gather(bf16[8,8,4]{1,0,2:T(8,128)(2,1)S(1)} %copy.43), channel_id=1, replica_groups=mesh['dap'=8,'seq'=4] {'dap'}, dimensions={2}, use_global_device_ids=true | all-gather | bytes 4608 | tf_op jit(solution)/shard_map/all_gather | solution.py:108
  34.0 0.7 %slice-done = bf16[1,8,256]{2,1,0:T(8,128)(2,1)S(1)} async-done(((bf16[1,8,1024]{2,1,0:T(8,128)(2,1)}), bf16[1,8,256]{2,1,0:T(8,128)(2,1)S(1)}, s32[]{:S(2)}) %slice-start) | async-done | bytes 4120 | tf_op jit(solution)/shard_map/slice | solution.py:117
  34.9 4.6 %collective-permute-done.1 = bf16[1,16,512]{2,1,0:T(8,128)(2,1)S(1)} collective-permute-done((bf16[1,16,512]{2,1,0:T(8,128)(2,1)S(1)}, bf16[1,16,512]{2,1,0:T(8,128)(2,1)S(1)}, u32[]{:S(2)}, u32[]{:S(2)}) %collective-permute-start.1) | collective-permute-done | bytes 16416 | tf_op jit(solution)/shard_map/ppermute | solution.py:15
  40.0 0.3 convolution_bitcast_fusion.1
  40.4 0.5 copy-done.3
  41.2 0.6 broadcast.233
  41.8 0.7 %reduce.5 = bf16[8,256]{1,0:T(8,128)(2,1)S(1)} reduce(bf16[8,1,1,256]{3,2,1,0:T(2,128)(2,1)S(1)} %bitcast.77, bf16[]{:T(256)} %broadcast.233), dimensions={1,2}, to_apply=%bitcast.76.reduce_sub_computation | reduce | bytes 8194
  42.5 0.6 reshape.311
  43.1 3.3 %all-to-all-start = ((bf16[8,2,128]{2,1,0:T(2,128)(2,1)}), bf16[8,2,128]{2,1,0:T(2,128)(2,1)S(1)}, u32[]{:S(2)}, u32[]{:S(2)}) async-start(bf16[8,2,128]{2,1,0:T(2,128)(2,1)} %reshape.311), calls=%async_computation | async-start | bytes 8192 | tf_op jit(solution)/shard_map/all_to_all | solution.py:158
  46.5 0.2 compare_reduce_fusion
  46.7 4.3 %all-to-all-done = bf16[8,2,128]{2,1,0:T(2,128)(2,1)S(1)} async-done(((bf16[8,2,128]{2,1,0:T(2,128)(2,1)}), bf16[8,2,128]{2,1,0:T(2,128)(2,1)S(1)}, u32[]{:S(2)}, u32[]{:S(2)}) %all-to-all-start) | async-done | bytes 4128 | tf_op jit(solution)/shard_map/all_to_all | solution.py:158
  51.1 0.2 fusion.40
  51.4 0.2 convolution_convert_fusion
  52.1 0.2 convolution_bitcast_fusion
  52.4 0.3 fusion.72
  52.7 0.2 multiply_reduce_fusion
  52.9 0.4 fusion.18
  53.3 0.7 %reduce.6 = bf16[8,256]{1,0:T(8,128)(2,1)S(1)} reduce(bf16[8,1,1,256]{3,0,2,1:T(8,128)(2,1)S(1)} %fusion.18, bf16[]{:T(256)} %broadcast.233), dimensions={1,2}, to_apply=%copy.55.reduce_sub_computation | reduce | bytes 8194 | tf_op jit(solution)/shard_map/broadcast_in_dim;transpose | solution.py:162
  54.1 7.1 %all_to_all.12 = bf16[8,2,128]{2,1,0:T(2,128)(2,1)S(1)} all-to-all(bf16[8,2,128]{2,1,0:T(2,128)(2,1)S(1)} %reshape.313), channel_id=1, replica_groups=mesh['dap'=8,'seq'=4] {'dap'}, dimensions={0} | all-to-all | bytes 8192 | tf_op jit(solution)/shard_map/all_to_all | solution.py:163
  61.1 0.6 copy.83
  (78 shorter events, 2.9 us)
Async XLA Ops:
  0.0 1.1 %copy-start = (bf16[256,1024]{1,0:T(8,128)(2,1)S(1)}, bf16[256,1024]{1,0:T(8,128)(2,1)}, u32[]{:S(2)}) copy-start(bf16[256,1024]{1,0:T(8,128)(2,1)} %param.16) | copy-start | bytes 1572868
  0.0 0.9 %copy-start.6 = (bf16[1,8,256]{2,1,0:T(8,128)(2,1)S(1)}, bf16[1,8,256]{2,1,0:T(8,128)(2,1)}, u32[]{:S(2)}) copy-start(bf16[1,8,256]{2,1,0:T(8,128)(2,1)} %param.12) | copy-start | bytes 12292
  1.3 22.7 %copy-start.7 = (bf16[1,8,1024]{2,1,0:T(8,128)(2,1)}, bf16[1,8,1024]{2,1,0:T(8,128)(2,1)S(1)}, u32[]{:S(2)}) copy-start(bf16[1,8,1024]{2,1,0:T(8,128)(2,1)S(1)} %fusion.12) | copy-start | bytes 49156
  1.3 3.1 %copy-start.12 = (s32[1,8]{1,0:T(1,128)S(1)}, s32[1,8]{1,0:T(1,128)}, u32[]{:S(2)}) copy-start(s32[1,8]{1,0:T(1,128)} %param.14) | copy-start | bytes 100
  1.3 33.4 %collective-permute-start = (bf16[1,8,512]{2,1,0:T(8,128)(2,1)S(1)}, bf16[1,8,512]{2,1,0:T(8,128)(2,1)S(1)}, u32[]{:S(2)}, u32[]{:S(2)}) collective-permute-start(bf16[1,8,512]{2,1,0:T(8,128)(2,1)S(1)} %get-tuple-element.45), channel_id=1, source_target_pairs={{0,1},{1,0},{2,3},{3,2},{4,5},{5,4},{6,7},{7,6},{8,9},{9,8},{10,11... | collective-permute-start | bytes 24584 | tf_op jit(solution)/shard_map/ppermute | solution.py:15
  5.1 38.0 %all-to-all-start.1 = ((bf16[1,8,1]{2,0,1:T(2,128)(2,1)}), bf16[1,8,1]{2,0,1:T(2,128)(2,1)S(1)}, u32[]{:S(2)}, u32[]{:S(2)}) async-start(bf16[1,8,1]{2,0,1:T(2,128)(2,1)} %copy.49), calls=%async_computation.1 | async-start | bytes 8192 | tf_op jit(solution)/shard_map/all_to_all | solution.py:159
  8.8 0.7 %copy-start.13 = (s32[32]{0:T(128)S(1)}, s32[32]{0:T(128)}, u32[]{:S(2)}) copy-start(s32[32]{0:T(128)} %param.15) | copy-start | bytes 388
  8.8 0.9 %copy-start.5 = (bf16[8,4,128]{2,1,0:T(4,128)(2,1)S(1)}, bf16[8,4,128]{2,1,0:T(4,128)(2,1)}, u32[]{:S(2)}) copy-start(bf16[8,4,128]{2,1,0:T(4,128)(2,1)} %param.13) | copy-start | bytes 24580
  10.1 0.7 %copy-start.9 = (f32[2,8]{1,0:T(2,128)S(1)}, f32[2,8]{1,0:T(2,128)}, u32[]{:S(2)}) copy-start(f32[2,8]{1,0:T(2,128)} %param.19) | copy-start | bytes 196
  10.7 0.7 %copy-start.14 = (u32[32]{0:T(128)S(1)}, u32[32]{0:T(128)}, u32[]{:S(2)}) copy-start(u32[32]{0:T(128)} %constant.102) | copy-start | bytes 388
  12.6 11.2 %copy-start.11 = (f32[128,8]{0,1:T(8,128)S(1)}, f32[128,8]{0,1:T(8,128)}, u32[]{:S(2)}) copy-start(f32[128,8]{0,1:T(8,128)} %param.18) | copy-start | bytes 12292
  34.0 0.7 %slice-start = ((bf16[1,8,1024]{2,1,0:T(8,128)(2,1)}), bf16[1,8,256]{2,1,0:T(8,128)(2,1)S(1)}, s32[]{:S(2)}) async-start(bf16[1,8,1024]{2,1,0:T(8,128)(2,1)} %copy-done.7), calls=%async_computation.3 | async-start | bytes 8192 | tf_op jit(solution)/shard_map/slice | solution.py:117
  34.8 4.7 %collective-permute-start.1 = (bf16[1,16,512]{2,1,0:T(8,128)(2,1)S(1)}, bf16[1,16,512]{2,1,0:T(8,128)(2,1)S(1)}, u32[]{:S(2)}, u32[]{:S(2)}) collective-permute-start(bf16[1,16,512]{2,1,0:T(8,128)(2,1)S(1)} %maximum_select_fusion.2), channel_id=1, source_target_pairs={{0,2},{1,3},{2,0},{3,1},{4,6},{5,7},{6,4},{7,5},{8,10},{9,11},{10,... | collective-permute-start | bytes 49160 | tf_op jit(solution)/shard_map/ppermute | solution.py:15
  34.9 16.5 %copy-start.10 = (bf16[256,1024]{1,0:T(8,128)(2,1)S(1)}, bf16[256,1024]{1,0:T(8,128)(2,1)}, u32[]{:S(2)}) copy-start(bf16[256,1024]{1,0:T(8,128)(2,1)} %param.20) | copy-start | bytes 1572868
  40.0 0.9 %copy-start.3 = (bf16[256,256]{1,0:T(8,128)(2,1)S(1)}, bf16[256,256]{1,0:T(8,128)(2,1)}, u32[]{:S(2)}) copy-start(bf16[256,256]{1,0:T(8,128)(2,1)} %param.17) | copy-start | bytes 393220
  40.3 0.7 %copy-start.8 = (bf16[1,8,1024]{2,1,0:T(8,128)(2,1)S(1)}, bf16[1,8,1024]{2,1,0:T(8,128)(2,1)}, u32[]{:S(2)}) copy-start(bf16[1,8,1024]{2,1,0:T(8,128)(2,1)} %copy-done.7) | copy-start | bytes 49156
  43.1 7.9 %all-to-all-start = ((bf16[8,2,128]{2,1,0:T(2,128)(2,1)}), bf16[8,2,128]{2,1,0:T(2,128)(2,1)S(1)}, u32[]{:S(2)}, u32[]{:S(2)}) async-start(bf16[8,2,128]{2,1,0:T(2,128)(2,1)} %reshape.311), calls=%async_computation | async-start | bytes 8192 | tf_op jit(solution)/shard_map/all_to_all | solution.py:158
  51.3 1.1 %copy-start.4 = (bf16[256,256]{1,0:T(8,128)(2,1)S(1)}, bf16[256,256]{1,0:T(8,128)(2,1)}, u32[]{:S(2)}) copy-start(bf16[256,256]{1,0:T(8,128)(2,1)} %param.21) | copy-start | bytes 393220
  51.4 1.6 %copy-start.2 = (bf16[256,1024]{1,0:T(8,128)(2,1)S(1)}, bf16[256,1024]{1,0:T(8,128)(2,1)}, u32[]{:S(2)}) copy-start(bf16[256,1024]{1,0:T(8,128)(2,1)} %param.22) | copy-start | bytes 1572868
  51.6 1.3 %copy-start.1 = (bf16[1024,256]{1,0:T(8,128)(2,1)S(1)}, bf16[1024,256]{1,0:T(8,128)(2,1)}, u32[]{:S(2)}) copy-start(bf16[1024,256]{1,0:T(8,128)(2,1)} %param.23) | copy-start | bytes 1572868
